TPU v7x, 256 devices: a whole 4x4x8 slice. The times are simulated.
256 devices in a mesh: row: 16 (over z_hi, y, core), col: 16 (over x, z_lo).
Axes of the slice: x: 4, y: 4, z: 8 (z_hi: 2, z_lo: 4; z = z_hi * 4 + z_lo), core: 2. Of those that a mesh axis runs over, the one named last changes fastest.
Arguments:
- act_sketch: bfloat16 [2, 8192, 256], P(None, 'row'), may hold values from -6 to 6
- grad_sketch: bfloat16 [2, 8192, 256], P(None, 'row'), may hold values from -6 to 6
- targets: float32 [8192, 256], P('row'), may hold values from -6 to 6
Outputs:
- residual: float32 [8192, 256], P(('row', 'col'))
All inputs are finite; a program needn't handle non-finite values.
Results may differ from a plain program's by a relative error of at most 0.014.
The roundings to bfloat16 on the way count: a program that leaves them out, or rounds other values in their place, can miss the bound.
Values may be sent and summed in bfloat16 or wider, within the bound.
A program may use at most 64 MiB of HBM per device.

v0:
```python
import math
import jax
import jax.numpy as jnp
from jax import lax
from jax.sharding import PartitionSpec as P

ITERS = 8


def broadcast(value, axis, source):
    kept = jnp.where(lax.axis_index(axis) == source, value, 0).astype(value.dtype)
    return lax.psum(kept, axis)


def spread(panel, root):
    return broadcast(panel, "row", root)


def gram_pair(left, right):
    return lax.dot_general(
        left, right, (((1,), (1,)), ((), ())), preferred_element_type=jnp.float32
    )


def body(act_sketch, grad_sketch, targets):
    row_count = lax.axis_size("row")
    col_count = lax.axis_size("col")
    ratio = col_count // row_count
    examples = targets.shape[0]
    col_block = examples // ratio
    share_rows = examples // col_count
    col_place = lax.axis_index("col")
    root = col_place // ratio
    scale = act_sketch.shape[2] * math.sqrt(examples * row_count) / 4.0
    act_cols, grad_cols = (broadcast(act_sketch, "row", root), broadcast(grad_sketch, "row", root))
    total = jnp.zeros((examples, col_block), jnp.float32)
    for layer in range(act_sketch.shape[0]):
        act_gram = gram_pair(act_sketch[layer], act_cols[layer])
        grad_gram = gram_pair(grad_sketch[layer], grad_cols[layer])
        total = total + act_gram * grad_gram
    kernel = (total / scale).astype(jnp.bfloat16)
    share = lax.dynamic_slice_in_dim(targets, col_place * share_rows, share_rows, 0)
    for step in range(ITERS):
        squashed = jnp.tanh(share).astype(jnp.bfloat16)
        gathered = lax.all_gather(squashed, "col", axis=0, tiled=True)
        panel = spread(gathered, root)
        partial_value = jnp.dot(kernel, panel, preferred_element_type=jnp.float32)
        piece = lax.psum_scatter(partial_value, "col", scatter_dimension=0, tiled=True)
        share = share - 0.05 * piece
    return share


def solution(mesh):
    return jax.shard_map(
        body,
        mesh=mesh,
        in_specs=(P(None, "row", None), P(None, "row", None), P("row", None)),
        out_specs=P(("row", "col"), None),
        check_vma=False,
    )
```

profile of v0, /device:TPU:8, one launch (start us, length us, event | category | flops | bytes accessed | tf_op | source)
XLA Modules:
  0.0 2479.9 jit_solution(18417355909062240451)
XLA Ops:
  6.5 0.8 tanh_convert_fusion.7
  7.4 46.0 %all_gather.24 = bf16[512,256]{1,0:T(8,128)(2,1)S(1)} all-gather(bf16[32,256]{1,0:T(8,128)(2,1)S(1)} %tanh_convert_fusion.7), channel_id=1, replica_groups=mesh['row'=16,'col'=16] {'col'}, dimensions={0}, use_global_device_ids=true | all-gather | bytes 278528 | tf_op jit(solution)/shard_map/all_gather | solution.py:45
  53.3 0.7 broadcast_select_fusion.9
  54.0 1.1 broadcast_select_fusion
  55.2 172.0 %all-reduce.24.cloned.1.call-done = (bf16[2,512,256]{2,1,0:T(8,128)(2,1)}, bf16[2,512,256]{2,1,0:T(8,128)(2,1)}, bf16[512,256]{1,0:T(8,128)(2,1)}) async-done(((bf16[2,512,256]{2,1,0:T(8,128)(2,1)}, bf16[2,512,256]{2,1,0:T(8,128)(2,1)}, bf16[512,256]{1,0:T(8,128)(2,1)}), (bf16[2,512,256]{2,1,0:T(8,128)(2,1)}, bf16[2,512,256]{2,1,0:T(8,128)(2,1)}, bf16[512,256]{1,0:T(8,128)(2,1)})) %all-reduce.24.cloned.1.call-update) | async-done | bytes 1310736 | tf_op jit(solution)/shard_map/psum | solution.py:12
  227.2 1.3 fusion.3
  230.9 1.1 fusion.13
  232.1 94.1 %reduce-scatter.9.cloned.1.call-done = f32[32,256]{1,0:T(8,128)} async-done(((f32[512,256]{1,0:T(8,128)}), f32[32,256]{1,0:T(8,128)}) %reduce-scatter.9.cloned.1.call-update) | async-done | bytes 32784 | tf_op jit(solution)/shard_map/reduce_scatter | solution.py:48
  326.2 0.8 tanh_convert_fusion.6
  327.0 39.1 %all_gather.25 = bf16[512,256]{1,0:T(8,128)(2,1)S(1)} all-gather(bf16[32,256]{1,0:T(8,128)(2,1)S(1)} %get-tuple-element.12), channel_id=1, replica_groups=mesh['row'=16,'col'=16] {'col'}, dimensions={0}, use_global_device_ids=true | all-gather | bytes 278528 | tf_op jit(solution)/shard_map/all_gather | solution.py:45
  366.2 0.7 broadcast_select_fusion.8
  367.0 169.6 %all-reduce.10.cloned.1.call-done = bf16[512,256]{1,0:T(8,128)(2,1)} async-done(((bf16[512,256]{1,0:T(8,128)(2,1)}), bf16[512,256]{1,0:T(8,128)(2,1)}) %all-reduce.10.cloned.1.call-update) | async-done | bytes 262160 | tf_op jit(solution)/shard_map/psum | solution.py:12
  536.6 2.1 fusion.14
  538.7 94.2 %reduce-scatter.11.cloned.1.call-done = f32[32,256]{1,0:T(8,128)} async-done(((f32[512,256]{1,0:T(8,128)}), f32[32,256]{1,0:T(8,128)}) %reduce-scatter.11.cloned.1.call-update) | async-done | bytes 32784 | tf_op jit(solution)/shard_map/reduce_scatter | solution.py:48
  633.0 0.8 tanh_convert_fusion.5
  633.8 39.5 %all_gather.26 = bf16[512,256]{1,0:T(8,128)(2,1)S(1)} all-gather(bf16[32,256]{1,0:T(8,128)(2,1)S(1)} %tanh_convert_fusion.5), channel_id=1, replica_groups=mesh['row'=16,'col'=16] {'col'}, dimensions={0}, use_global_device_ids=true | all-gather | bytes 278528 | tf_op jit(solution)/shard_map/all_gather | solution.py:45
  673.2 0.7 broadcast_select_fusion.7
  674.0 169.0 %all-reduce.12.cloned.1.call-done = bf16[512,256]{1,0:T(8,128)(2,1)} async-done(((bf16[512,256]{1,0:T(8,128)(2,1)}), bf16[512,256]{1,0:T(8,128)(2,1)}) %all-reduce.12.cloned.1.call-update) | async-done | bytes 262160 | tf_op jit(solution)/shard_map/psum | solution.py:12
  843.0 2.1 fusion.15
  845.2 94.2 %reduce-scatter.13.cloned.1.call-done = f32[32,256]{1,0:T(8,128)} async-done(((f32[512,256]{1,0:T(8,128)}), f32[32,256]{1,0:T(8,128)}) %reduce-scatter.13.cloned.1.call-update) | async-done | bytes 32784 | tf_op jit(solution)/shard_map/reduce_scatter | solution.py:48
  939.4 0.8 tanh_convert_fusion.4
  940.2 39.5 %all_gather.27 = bf16[512,256]{1,0:T(8,128)(2,1)S(1)} all-gather(bf16[32,256]{1,0:T(8,128)(2,1)S(1)} %get-tuple-element.10), channel_id=1, replica_groups=mesh['row'=16,'col'=16] {'col'}, dimensions={0}, use_global_device_ids=true | all-gather | bytes 278528 | tf_op jit(solution)/shard_map/all_gather | solution.py:45
  979.7 0.7 broadcast_select_fusion.6
  980.5 169.0 %all-reduce.14.cloned.1.call-done = bf16[512,256]{1,0:T(8,128)(2,1)} async-done(((bf16[512,256]{1,0:T(8,128)(2,1)}), bf16[512,256]{1,0:T(8,128)(2,1)}) %all-reduce.14.cloned.1.call-update) | async-done | bytes 262160 | tf_op jit(solution)/shard_map/psum | solution.py:12
  1149.5 2.1 fusion.16
  1151.6 94.4 %reduce-scatter.15.cloned.1.call-done = f32[32,256]{1,0:T(8,128)} async-done(((f32[512,256]{1,0:T(8,128)}), f32[32,256]{1,0:T(8,128)}) %reduce-scatter.15.cloned.1.call-update) | async-done | bytes 32784 | tf_op jit(solution)/shard_map/reduce_scatter | solution.py:48
  1246.1 0.8 tanh_convert_fusion.3
  1246.8 39.5 %all_gather.28 = bf16[512,256]{1,0:T(8,128)(2,1)S(1)} all-gather(bf16[32,256]{1,0:T(8,128)(2,1)S(1)} %tanh_convert_fusion.3), channel_id=1, replica_groups=mesh['row'=16,'col'=16] {'col'}, dimensions={0}, use_global_device_ids=true | all-gather | bytes 278528 | tf_op jit(solution)/shard_map/all_gather | solution.py:45
  1286.3 0.7 broadcast_select_fusion.5
  1287.1 169.2 %all-reduce.16.cloned.1.call-done = bf16[512,256]{1,0:T(8,128)(2,1)} async-done(((bf16[512,256]{1,0:T(8,128)(2,1)}), bf16[512,256]{1,0:T(8,128)(2,1)}) %all-reduce.16.cloned.1.call-update) | async-done | bytes 262160 | tf_op jit(solution)/shard_map/psum | solution.py:12
  1456.3 2.1 fusion.17
  1458.5 94.2 %reduce-scatter.17.cloned.1.call-done = f32[32,256]{1,0:T(8,128)} async-done(((f32[512,256]{1,0:T(8,128)}), f32[32,256]{1,0:T(8,128)}) %reduce-scatter.17.cloned.1.call-update) | async-done | bytes 32784 | tf_op jit(solution)/shard_map/reduce_scatter | solution.py:48
  1552.7 0.8 tanh_convert_fusion.2
  1553.5 39.5 %all_gather.29 = bf16[512,256]{1,0:T(8,128)(2,1)S(1)} all-gather(bf16[32,256]{1,0:T(8,128)(2,1)S(1)} %get-tuple-element.8), channel_id=1, replica_groups=mesh['row'=16,'col'=16] {'col'}, dimensions={0}, use_global_device_ids=true | all-gather | bytes 278528 | tf_op jit(solution)/shard_map/all_gather | solution.py:45
  1593.7 169.0 %all-reduce.18.cloned.1.call-done = bf16[512,256]{1,0:T(8,128)(2,1)} async-done(((bf16[512,256]{1,0:T(8,128)(2,1)}), bf16[512,256]{1,0:T(8,128)(2,1)}) %all-reduce.18.cloned.1.call-update) | async-done | bytes 262160 | tf_op jit(solution)/shard_map/psum | solution.py:12
  1762.8 2.1 fusion.18
  1764.9 94.2 %reduce-scatter.19.cloned.1.call-done = f32[32,256]{1,0:T(8,128)} async-done(((f32[512,256]{1,0:T(8,128)}), f32[32,256]{1,0:T(8,128)}) %reduce-scatter.19.cloned.1.call-update) | async-done | bytes 32784 | tf_op jit(solution)/shard_map/reduce_scatter | solution.py:48
  1859.2 0.8 tanh_convert_fusion.1
  1859.9 39.5 %all_gather.30 = bf16[512,256]{1,0:T(8,128)(2,1)S(1)} all-gather(bf16[32,256]{1,0:T(8,128)(2,1)S(1)} %tanh_convert_fusion.1), channel_id=1, replica_groups=mesh['row'=16,'col'=16] {'col'}, dimensions={0}, use_global_device_ids=true | all-gather | bytes 278528 | tf_op jit(solution)/shard_map/all_gather | solution.py:45
  1900.2 169.0 %all-reduce.20.cloned.1.call-done = bf16[512,256]{1,0:T(8,128)(2,1)} async-done(((bf16[512,256]{1,0:T(8,128)(2,1)}), bf16[512,256]{1,0:T(8,128)(2,1)}) %all-reduce.20.cloned.1.call-update) | async-done | bytes 262160 | tf_op jit(solution)/shard_map/psum | solution.py:12
  2069.2 2.1 fusion.19
  2071.4 94.2 %reduce-scatter.21.cloned.1.call-done = f32[32,256]{1,0:T(8,128)} async-done(((f32[512,256]{1,0:T(8,128)}), f32[32,256]{1,0:T(8,128)}) %reduce-scatter.21.cloned.1.call-update) | async-done | bytes 32784 | tf_op jit(solution)/shard_map/reduce_scatter | solution.py:48
  2165.6 0.8 tanh_convert_fusion
  2166.4 39.5 %all_gather.31 = bf16[512,256]{1,0:T(8,128)(2,1)S(1)} all-gather(bf16[32,256]{1,0:T(8,128)(2,1)S(1)} %tanh_convert_fusion), channel_id=1, replica_groups=mesh['row'=16,'col'=16] {'col'}, dimensions={0}, use_global_device_ids=true | all-gather | bytes 278528 | tf_op jit(solution)/shard_map/all_gather | solution.py:45
  2206.6 169.0 %all-reduce.22.cloned.1.call-done = bf16[512,256]{1,0:T(8,128)(2,1)} async-done(((bf16[512,256]{1,0:T(8,128)(2,1)}), bf16[512,256]{1,0:T(8,128)(2,1)}) %all-reduce.22.cloned.1.call-update) | async-done | bytes 262160 | tf_op jit(solution)/shard_map/psum | solution.py:12
  2375.7 2.1 fusion.20
  2377.8 94.2 %reduce-scatter.23.cloned.1.call-done = f32[32,256]{1,0:T(8,128)} async-done(((f32[512,256]{1,0:T(8,128)}), f32[32,256]{1,0:T(8,128)}) %reduce-scatter.23.cloned.1.call-update) | async-done | bytes 32784 | tf_op jit(solution)/shard_map/reduce_scatter | solution.py:48
  2472.0 1.4 multiply_subtract_fusion
  (56 shorter events, 5.4 us)
Async XLA Ops:
  6.5 47.5 %copy-start = (bf16[2,512,256]{2,1,0:T(8,128)(2,1)S(1)}, bf16[2,512,256]{2,1,0:T(8,128)(2,1)}, u32[]{:S(2)}) copy-start(bf16[2,512,256]{2,1,0:T(8,128)(2,1)} %param.4) | copy-start | bytes 1572868
  6.5 220.7 %all-reduce.24.cloned.1.call-start = ((), (), s32[]{:S(2)}) async-start(), calls=%async_computation.23 | async-start | bytes 2621440 | tf_op jit(solution)/shard_map/psum | solution.py:12
  55.1 172.1 %copy-start.1 = (bf16[2,512,256]{2,1,0:T(8,128)(2,1)S(1)}, bf16[2,512,256]{2,1,0:T(8,128)(2,1)}, u32[]{:S(2)}) copy-start(bf16[2,512,256]{2,1,0:T(8,128)(2,1)} %param.3) | copy-start | bytes 1572868
  55.1 271.1 %reduce-scatter.9.cloned.1.call-start = ((), (), s32[]{:S(2)}) async-start(), calls=%async_computation.8 | async-start | bytes 557056 | tf_op jit(solution)/shard_map/reduce_scatter | solution.py:48
  227.2 1.4 copy-start.3
  228.6 1.0 copy-start.2
  230.0 1.0 copy-start.5
  232.1 304.5 %all-reduce.10.cloned.1.call-start = ((), (), s32[]{:S(2)}) async-start(), calls=%async_computation.9 | async-start | bytes 524288 | tf_op jit(solution)/shard_map/psum | solution.py:12
  366.9 266.1 %reduce-scatter.11.cloned.1.call-start = ((), (), s32[]{:S(2)}) async-start(), calls=%async_computation.10 | async-start | bytes 557056 | tf_op jit(solution)/shard_map/reduce_scatter | solution.py:48
  538.7 304.3 %all-reduce.12.cloned.1.call-start = ((), (), s32[]{:S(2)}) async-start(), calls=%async_computation.11 | async-start | bytes 524288 | tf_op jit(solution)/shard_map/psum | solution.py:12
  674.0 265.5 %reduce-scatter.13.cloned.1.call-start = ((), (), s32[]{:S(2)}) async-start(), calls=%async_computation.12 | async-start | bytes 557056 | tf_op jit(solution)/shard_map/reduce_scatter | solution.py:48
  845.1 94.3 %copy-start.7 = (f32[32,256]{1,0:T(8,128)S(1)}, f32[32,256]{1,0:T(8,128)}, u32[]{:S(2)}) copy-start(f32[32,256]{1,0:T(8,128)} %reduce-scatter.11.cloned.1.call-done) | copy-start | bytes 98308
  845.1 304.4 %all-reduce.14.cloned.1.call-start = ((), (), s32[]{:S(2)}) async-start(), calls=%async_computation.13 | async-start | bytes 524288 | tf_op jit(solution)/shard_map/psum | solution.py:12
  980.4 265.6 %reduce-scatter.15.cloned.1.call-start = ((), (), s32[]{:S(2)}) async-start(), calls=%async_computation.14 | async-start | bytes 557056 | tf_op jit(solution)/shard_map/reduce_scatter | solution.py:48
  1151.6 304.7 %all-reduce.16.cloned.1.call-start = ((), (), s32[]{:S(2)}) async-start(), calls=%async_computation.15 | async-start | bytes 524288 | tf_op jit(solution)/shard_map/psum | solution.py:12
  1287.1 265.7 %reduce-scatter.17.cloned.1.call-start = ((), (), s32[]{:S(2)}) async-start(), calls=%async_computation.16 | async-start | bytes 557056 | tf_op jit(solution)/shard_map/reduce_scatter | solution.py:48
  1458.4 94.3 %copy-start.8 = (f32[32,256]{1,0:T(8,128)S(1)}, f32[32,256]{1,0:T(8,128)}, u32[]{:S(2)}) copy-start(f32[32,256]{1,0:T(8,128)} %reduce-scatter.15.cloned.1.call-done) | copy-start | bytes 98308
  1458.4 304.3 %all-reduce.18.cloned.1.call-start = ((), (), s32[]{:S(2)}) async-start(), calls=%async_computation.17 | async-start | bytes 524288 | tf_op jit(solution)/shard_map/psum | solution.py:12
  1593.7 265.5 %reduce-scatter.19.cloned.1.call-start = ((), (), s32[]{:S(2)}) async-start(), calls=%async_computation.18 | async-start | bytes 557056 | tf_op jit(solution)/shard_map/reduce_scatter | solution.py:48
  1764.9 304.3 %all-reduce.20.cloned.1.call-start = ((), (), s32[]{:S(2)}) async-start(), calls=%async_computation.19 | async-start | bytes 524288 | tf_op jit(solution)/shard_map/psum | solution.py:12
  1900.1 265.5 %reduce-scatter.21.cloned.1.call-start = ((), (), s32[]{:S(2)}) async-start(), calls=%async_computation.20 | async-start | bytes 557056 | tf_op jit(solution)/shard_map/reduce_scatter | solution.py:48
  2071.3 94.3 %copy-start.4 = (f32[32,256]{1,0:T(8,128)S(1)}, f32[32,256]{1,0:T(8,128)}, u32[]{:S(2)}) copy-start(f32[32,256]{1,0:T(8,128)} %reduce-scatter.19.cloned.1.call-done) | copy-start | bytes 98308
  2071.3 304.3 %all-reduce.22.cloned.1.call-start = ((), (), s32[]{:S(2)}) async-start(), calls=%async_computation.21 | async-start | bytes 524288 | tf_op jit(solution)/shard_map/psum | solution.py:12
  2206.6 265.4 %reduce-scatter.23.cloned.1.call-start = ((), (), s32[]{:S(2)}) async-start(), calls=%async_computation.22 | async-start | bytes 557056 | tf_op jit(solution)/shard_map/reduce_scatter | solution.py:48
  2377.7 94.2 %copy-start.6 = (f32[32,256]{1,0:T(8,128)S(1)}, f32[32,256]{1,0:T(8,128)}, u32[]{:S(2)}) copy-start(f32[32,256]{1,0:T(8,128)} %reduce-scatter.21.cloned.1.call-done) | copy-start | bytes 98308
Sparse Core Ops, SparseCore 0:
  55.3 171.9 all-reduce.23
  232.2 93.9 reduce-scatter.8
  367.0 169.5 all-reduce.9
  538.9 93.9 reduce-scatter.10
  674.1 168.9 all-reduce.11
  845.4 93.9 reduce-scatter.12
  980.5 168.9 all-reduce.13
  1152.0 94.0 reduce-scatter.14
  1287.2 169.1 all-reduce.15
  1458.7 93.9 reduce-scatter.16
  1593.8 168.9 all-reduce.17
  1765.1 93.9 reduce-scatter.18
  1900.3 168.9 all-reduce.19
  2071.6 93.9 reduce-scatter.20
  2206.7 168.9 all-reduce.21
  2378.0 93.9 reduce-scatter.22
where the time goes:
time: 2480 us
  waiting for transfers between devices  2110 us (85%)
  blocking collectives  322 us (13%)
    psum x8, waiting for transfers between devices, broadcast(): return lax.psum(kept, axis)  1360 us
    reduce_scatter x8, waiting for transfers between devices, body(): lax.psum_scatter(partial_value, 'col', scatter_dimension=0, tiled=True)  754 us
    all_gather x8, blocking collectives, body(): gathered = lax.all_gather(squashed, 'col', axis=0, tiled=True)  322 us
  transfers between devices with their start and end apart: 16, of which 16 were waited for; matrix products, arithmetic and copies ran while one was open for 0% of the time, Pallas kernels for 0%

commit v1 on v0

--- a/solution.py
+++ b/solution.py
@@ -9,7 +9,7 @@
 
 def broadcast(value, axis, source):
     kept = jnp.where(lax.axis_index(axis) == source, value, 0).astype(value.dtype)
-    return lax.psum(kept, axis)
+    return jnp.sum(lax.all_gather(kept, axis_name=axis), axis=0)
 
 
 def spread(panel, root):

time: 2480 us -> 1860 us (0.75)
  waiting for transfers between devices: 2110 us -> 1460 us
  other arithmetic: 14.5 us -> 47.7 us
    psum x8 -> x0, waiting for transfers between devices: 1360 us -> none  [broadcast(): return lax.psum(kept, axis)]
    all_gather x0 -> x10, waiting for transfers between devices: none -> 803 us  [broadcast(): return jnp.sum(lax.all_gather(kept, axis_name=axis), axis=0)]
    reduce_scatter x8, waiting for transfers between devices: 754 us -> 655 us  [body(): lax.psum_scatter(partial_value, 'col', scatter_dimension=0, tiled=True)]
    reduce_sum x0 -> x10, other arithmetic: none -> 32.4 us  [broadcast(): return jnp.sum(lax.all_gather(kept, axis_name=axis), axis=0)]
  transfers between devices with their start and end apart: 16 -> 18, of which waited for: 16 -> 18; matrix products, arithmetic and copies ran while one was open for 0% -> 1% of each run, Pallas kernels for 0% -> 0%
where the time goes in v1:
time: 1860 us; the launch traced here: 1850 us
  waiting for transfers between devices  1460 us (78%)
  blocking collectives  322 us (17%)
  other arithmetic  47.7 us (3%)
    all_gather x10, waiting for transfers between devices, broadcast(): return jnp.sum(lax.all_gather(kept, axis_name=axis), axis=0)  803 us
    reduce_scatter x8, waiting for transfers between devices, body(): lax.psum_scatter(partial_value, 'col', scatter_dimension=0, tiled=True)  655 us
    all_gather x8, blocking collectives, body(): gathered = lax.all_gather(squashed, 'col', axis=0, tiled=True)  322 us
  transfers between devices with their start and end apart: 18, of which 18 were waited for; matrix products, arithmetic and copies ran while one was open for 1% of the time, Pallas kernels for 0%

profile of v1, /device:TPU:8, one launch (start us, length us, event | category | flops | bytes accessed | tf_op | source)
XLA Modules:
  0.0 1854.4 jit_solution(10379672264522985195)
XLA Ops:
  7.3 46.0 %all_gather.88 = bf16[512,256]{1,0:T(8,128)(2,1)S(1)} all-gather(bf16[32,256]{1,0:T(8,128)(2,1)S(1)} %tanh_convert_fusion.7), channel_id=1, replica_groups=mesh['row'=16,'col'=16] {'col'}, dimensions={0}, use_global_device_ids=true | all-gather | bytes 278528 | tf_op jit(solution)/shard_map/all_gather | solution.py:45
  54.1 0.9 broadcast_select_fusion.1
  55.0 0.9 broadcast_select_fusion
  55.9 72.7 %all-gather.25.cloned.1.call-done = bf16[8192,256]{1,0:T(8,128)(2,1)} async-done(((bf16[512,256]{1,0:T(8,128)(2,1)}), bf16[8192,256]{1,0:T(8,128)(2,1)}) %all-gather.25.cloned.1.call-update) | async-done | bytes 4194320 | tf_op jit(solution)/shard_map/all_gather | solution.py:12
  128.6 2.9 reduce_sum.122
  131.5 102.9 %all-gather.21.cloned.1.call-done = bf16[32,512,256]{2,1,0:T(8,128)(2,1)} async-done(((bf16[2,512,256]{2,1,0:T(8,128)(2,1)}), bf16[32,512,256]{2,1,0:T(8,128)(2,1)}) %all-gather.21.cloned.1.call-update) | async-done | bytes 8388624 | tf_op jit(solution)/shard_map/all_gather | solution.py:12
  234.4 4.8 reduce_sum.120
  239.9 100.1 %all-gather.23.cloned.1.call-done = bf16[32,512,256]{2,1,0:T(8,128)(2,1)} async-done(((bf16[2,512,256]{2,1,0:T(8,128)(2,1)}), bf16[32,512,256]{2,1,0:T(8,128)(2,1)}) %all-gather.23.cloned.1.call-update) | async-done | bytes 8388624 | tf_op jit(solution)/shard_map/all_gather | solution.py:12
  340.0 4.8 reduce_sum.121
  345.2 1.3 fusion.2
  346.5 1.1 fusion.13
  347.7 81.6 %reduce-scatter.9.cloned.1.call-done = f32[32,256]{1,0:T(8,128)} async-done(((f32[512,256]{1,0:T(8,128)}), f32[32,256]{1,0:T(8,128)}) %reduce-scatter.9.cloned.1.call-update) | async-done | bytes 32784 | tf_op jit(solution)/shard_map/reduce_scatter | solution.py:48
  430.1 39.5 %all_gather.91 = bf16[512,256]{1,0:T(8,128)(2,1)S(1)} all-gather(bf16[32,256]{1,0:T(8,128)(2,1)S(1)} %get-tuple-element.9), channel_id=1, replica_groups=mesh['row'=16,'col'=16] {'col'}, dimensions={0}, use_global_device_ids=true | all-gather | bytes 278528 | tf_op jit(solution)/shard_map/all_gather | solution.py:45
  470.4 75.4 %all-gather.27.cloned.1.call-done = bf16[8192,256]{1,0:T(8,128)(2,1)} async-done(((bf16[512,256]{1,0:T(8,128)(2,1)}), bf16[8192,256]{1,0:T(8,128)(2,1)}) %all-gather.27.cloned.1.call-update) | async-done | bytes 4194320 | tf_op jit(solution)/shard_map/all_gather | solution.py:12
  545.8 2.9 reduce_sum.123
  548.7 1.1 fusion.14
  549.9 81.9 %reduce-scatter.11.cloned.1.call-done = f32[32,256]{1,0:T(8,128)} async-done(((f32[512,256]{1,0:T(8,128)}), f32[32,256]{1,0:T(8,128)}) %reduce-scatter.11.cloned.1.call-update) | async-done | bytes 32784 | tf_op jit(solution)/shard_map/reduce_scatter | solution.py:48
  632.6 39.5 %all_gather.94 = bf16[512,256]{1,0:T(8,128)(2,1)S(1)} all-gather(bf16[32,256]{1,0:T(8,128)(2,1)S(1)} %tanh_convert_fusion.5), channel_id=1, replica_groups=mesh['row'=16,'col'=16] {'col'}, dimensions={0}, use_global_device_ids=true | all-gather | bytes 278528 | tf_op jit(solution)/shard_map/all_gather | solution.py:45
  672.9 75.2 %all-gather.29.cloned.1.call-done = bf16[8192,256]{1,0:T(8,128)(2,1)} async-done(((bf16[512,256]{1,0:T(8,128)(2,1)}), bf16[8192,256]{1,0:T(8,128)(2,1)}) %all-gather.29.cloned.1.call-update) | async-done | bytes 4194320 | tf_op jit(solution)/shard_map/all_gather | solution.py:12
  748.2 2.9 reduce_sum.124
  751.0 1.1 fusion.15
  752.3 82.0 %reduce-scatter.13.cloned.1.call-done = f32[32,256]{1,0:T(8,128)} async-done(((f32[512,256]{1,0:T(8,128)}), f32[32,256]{1,0:T(8,128)}) %reduce-scatter.13.cloned.1.call-update) | async-done | bytes 32784 | tf_op jit(solution)/shard_map/reduce_scatter | solution.py:48
  835.0 39.3 %all_gather.97 = bf16[512,256]{1,0:T(8,128)(2,1)S(1)} all-gather(bf16[32,256]{1,0:T(8,128)(2,1)S(1)} %get-tuple-element.7), channel_id=1, replica_groups=mesh['row'=16,'col'=16] {'col'}, dimensions={0}, use_global_device_ids=true | all-gather | bytes 278528 | tf_op jit(solution)/shard_map/all_gather | solution.py:45
  875.1 75.3 %all-gather.31.cloned.1.call-done = bf16[8192,256]{1,0:T(8,128)(2,1)} async-done(((bf16[512,256]{1,0:T(8,128)(2,1)}), bf16[8192,256]{1,0:T(8,128)(2,1)}) %all-gather.31.cloned.1.call-update) | async-done | bytes 4194320 | tf_op jit(solution)/shard_map/all_gather | solution.py:12
  950.4 2.9 reduce_sum.125
  953.3 1.1 fusion.16
  954.5 81.9 %reduce-scatter.15.cloned.1.call-done = f32[32,256]{1,0:T(8,128)} async-done(((f32[512,256]{1,0:T(8,128)}), f32[32,256]{1,0:T(8,128)}) %reduce-scatter.15.cloned.1.call-update) | async-done | bytes 32784 | tf_op jit(solution)/shard_map/reduce_scatter | solution.py:48
  1037.2 39.3 %all_gather.100 = bf16[512,256]{1,0:T(8,128)(2,1)S(1)} all-gather(bf16[32,256]{1,0:T(8,128)(2,1)S(1)} %tanh_convert_fusion.3), channel_id=1, replica_groups=mesh['row'=16,'col'=16] {'col'}, dimensions={0}, use_global_device_ids=true | all-gather | bytes 278528 | tf_op jit(solution)/shard_map/all_gather | solution.py:45
  1077.3 75.6 %all-gather.33.cloned.1.call-done = bf16[8192,256]{1,0:T(8,128)(2,1)} async-done(((bf16[512,256]{1,0:T(8,128)(2,1)}), bf16[8192,256]{1,0:T(8,128)(2,1)}) %all-gather.33.cloned.1.call-update) | async-done | bytes 4194320 | tf_op jit(solution)/shard_map/all_gather | solution.py:12
  1152.9 2.9 reduce_sum.126
  1155.8 1.1 fusion.17
  1157.0 81.9 %reduce-scatter.17.cloned.1.call-done = f32[32,256]{1,0:T(8,128)} async-done(((f32[512,256]{1,0:T(8,128)}), f32[32,256]{1,0:T(8,128)}) %reduce-scatter.17.cloned.1.call-update) | async-done | bytes 32784 | tf_op jit(solution)/shard_map/reduce_scatter | solution.py:48
  1239.6 39.6 %all_gather.103 = bf16[512,256]{1,0:T(8,128)(2,1)S(1)} all-gather(bf16[32,256]{1,0:T(8,128)(2,1)S(1)} %get-tuple-element.5), channel_id=1, replica_groups=mesh['row'=16,'col'=16] {'col'}, dimensions={0}, use_global_device_ids=true | all-gather | bytes 278528 | tf_op jit(solution)/shard_map/all_gather | solution.py:45
  1280.0 75.2 %all-gather.35.cloned.1.call-done = bf16[8192,256]{1,0:T(8,128)(2,1)} async-done(((bf16[512,256]{1,0:T(8,128)(2,1)}), bf16[8192,256]{1,0:T(8,128)(2,1)}) %all-gather.35.cloned.1.call-update) | async-done | bytes 4194320 | tf_op jit(solution)/shard_map/all_gather | solution.py:12
  1355.1 2.9 reduce_sum.127
  1358.0 1.1 fusion.18
  1359.2 81.8 %reduce-scatter.19.cloned.1.call-done = f32[32,256]{1,0:T(8,128)} async-done(((f32[512,256]{1,0:T(8,128)}), f32[32,256]{1,0:T(8,128)}) %reduce-scatter.19.cloned.1.call-update) | async-done | bytes 32784 | tf_op jit(solution)/shard_map/reduce_scatter | solution.py:48
  1441.9 39.7 %all_gather.106 = bf16[512,256]{1,0:T(8,128)(2,1)S(1)} all-gather(bf16[32,256]{1,0:T(8,128)(2,1)S(1)} %tanh_convert_fusion.1), channel_id=1, replica_groups=mesh['row'=16,'col'=16] {'col'}, dimensions={0}, use_global_device_ids=true | all-gather | bytes 278528 | tf_op jit(solution)/shard_map/all_gather | solution.py:45
  1482.4 75.4 %all-gather.37.cloned.1.call-done = bf16[8192,256]{1,0:T(8,128)(2,1)} async-done(((bf16[512,256]{1,0:T(8,128)(2,1)}), bf16[8192,256]{1,0:T(8,128)(2,1)}) %all-gather.37.cloned.1.call-update) | async-done | bytes 4194320 | tf_op jit(solution)/shard_map/all_gather | solution.py:12
  1557.7 2.9 reduce_sum.128
  1560.6 1.1 fusion.19
  1561.8 81.9 %reduce-scatter.21.cloned.1.call-done = f32[32,256]{1,0:T(8,128)} async-done(((f32[512,256]{1,0:T(8,128)}), f32[32,256]{1,0:T(8,128)}) %reduce-scatter.21.cloned.1.call-update) | async-done | bytes 32784 | tf_op jit(solution)/shard_map/reduce_scatter | solution.py:48
  1644.6 39.3 %all_gather.109 = bf16[512,256]{1,0:T(8,128)(2,1)S(1)} all-gather(bf16[32,256]{1,0:T(8,128)(2,1)S(1)} %tanh_convert_fusion), channel_id=1, replica_groups=mesh['row'=16,'col'=16] {'col'}, dimensions={0}, use_global_device_ids=true | all-gather | bytes 278528 | tf_op jit(solution)/shard_map/all_gather | solution.py:45
  1684.7 75.6 %all-gather.39.cloned.1.call-done = bf16[8192,256]{1,0:T(8,128)(2,1)} async-done(((bf16[512,256]{1,0:T(8,128)(2,1)}), bf16[8192,256]{1,0:T(8,128)(2,1)}) %all-gather.39.cloned.1.call-update) | async-done | bytes 4194320 | tf_op jit(solution)/shard_map/all_gather | solution.py:12
  1760.3 2.9 reduce_sum.129
  1763.2 1.1 fusion.20
  1764.3 81.8 %reduce-scatter.23.cloned.1.call-done = f32[32,256]{1,0:T(8,128)} async-done(((f32[512,256]{1,0:T(8,128)}), f32[32,256]{1,0:T(8,128)}) %reduce-scatter.23.cloned.1.call-update) | async-done | bytes 32784 | tf_op jit(solution)/shard_map/reduce_scatter | solution.py:48
  1846.2 1.4 multiply_subtract_fusion
  (67 shorter events, 14.3 us)
Async XLA Ops:
  6.5 122.1 %all-gather.25.cloned.1.call-start = ((), (), s32[]{:S(2)}) async-start(), calls=%async_computation.18 | async-start | bytes 4456448 | tf_op jit(solution)/shard_map/all_gather | solution.py:12
  54.0 180.4 %all-gather.21.cloned.1.call-start = ((), (), s32[]{:S(2)}) async-start(), calls=%async_computation.16 | async-start | bytes 8912896 | tf_op jit(solution)/shard_map/all_gather | solution.py:12
  55.0 285.1 %all-gather.23.cloned.1.call-start = ((), (), s32[]{:S(2)}) async-start(), calls=%async_computation.17 | async-start | bytes 8912896 | tf_op jit(solution)/shard_map/all_gather | solution.py:12
  55.9 373.4 %reduce-scatter.9.cloned.1.call-start = ((), (), s32[]{:S(2)}) async-start(), calls=%async_computation.8 | async-start | bytes 557056 | tf_op jit(solution)/shard_map/reduce_scatter | solution.py:48
  234.4 4.8 copy-start.1
  340.0 4.8 copy-start
  347.6 198.2 %all-gather.27.cloned.1.call-start = ((), (), s32[]{:S(2)}) async-start(), calls=%async_computation.19 | async-start | bytes 4456448 | tf_op jit(solution)/shard_map/all_gather | solution.py:12
  470.3 161.4 %reduce-scatter.11.cloned.1.call-start = ((), (), s32[]{:S(2)}) async-start(), calls=%async_computation.9 | async-start | bytes 557056 | tf_op jit(solution)/shard_map/reduce_scatter | solution.py:48
  549.8 198.3 %all-gather.29.cloned.1.call-start = ((), (), s32[]{:S(2)}) async-start(), calls=%async_computation.20 | async-start | bytes 4456448 | tf_op jit(solution)/shard_map/all_gather | solution.py:12
  631.8 202.5 %copy-start.4 = (f32[32,256]{1,0:T(8,128)S(1)}, f32[32,256]{1,0:T(8,128)}, u32[]{:S(2)}) copy-start(f32[32,256]{1,0:T(8,128)} %reduce-scatter.11.cloned.1.call-done) | copy-start | bytes 98308
  672.9 161.3 %reduce-scatter.13.cloned.1.call-start = ((), (), s32[]{:S(2)}) async-start(), calls=%async_computation.10 | async-start | bytes 557056 | tf_op jit(solution)/shard_map/reduce_scatter | solution.py:48
  752.2 198.2 %all-gather.31.cloned.1.call-start = ((), (), s32[]{:S(2)}) async-start(), calls=%async_computation.21 | async-start | bytes 4456448 | tf_op jit(solution)/shard_map/all_gather | solution.py:12
  875.1 161.3 %reduce-scatter.15.cloned.1.call-start = ((), (), s32[]{:S(2)}) async-start(), calls=%async_computation.11 | async-start | bytes 557056 | tf_op jit(solution)/shard_map/reduce_scatter | solution.py:48
  954.4 198.5 %all-gather.33.cloned.1.call-start = ((), (), s32[]{:S(2)}) async-start(), calls=%async_computation.22 | async-start | bytes 4456448 | tf_op jit(solution)/shard_map/all_gather | solution.py:12
  1036.4 202.5 %copy-start.5 = (f32[32,256]{1,0:T(8,128)S(1)}, f32[32,256]{1,0:T(8,128)}, u32[]{:S(2)}) copy-start(f32[32,256]{1,0:T(8,128)} %reduce-scatter.15.cloned.1.call-done) | copy-start | bytes 98308
  1077.3 161.6 %reduce-scatter.17.cloned.1.call-start = ((), (), s32[]{:S(2)}) async-start(), calls=%async_computation.12 | async-start | bytes 557056 | tf_op jit(solution)/shard_map/reduce_scatter | solution.py:48
  1156.9 198.2 %all-gather.35.cloned.1.call-start = ((), (), s32[]{:S(2)}) async-start(), calls=%async_computation.23 | async-start | bytes 4456448 | tf_op jit(solution)/shard_map/all_gather | solution.py:12
  1279.9 161.1 %reduce-scatter.19.cloned.1.call-start = ((), (), s32[]{:S(2)}) async-start(), calls=%async_computation.13 | async-start | bytes 557056 | tf_op jit(solution)/shard_map/reduce_scatter | solution.py:48
  1359.2 198.6 %all-gather.37.cloned.1.call-start = ((), (), s32[]{:S(2)}) async-start(), calls=%async_computation.24 | async-start | bytes 4456448 | tf_op jit(solution)/shard_map/all_gather | solution.py:12
  1441.0 202.7 %copy-start.2 = (f32[32,256]{1,0:T(8,128)S(1)}, f32[32,256]{1,0:T(8,128)}, u32[]{:S(2)}) copy-start(f32[32,256]{1,0:T(8,128)} %reduce-scatter.19.cloned.1.call-done) | copy-start | bytes 98308
  1482.3 161.4 %reduce-scatter.21.cloned.1.call-start = ((), (), s32[]{:S(2)}) async-start(), calls=%async_computation.14 | async-start | bytes 557056 | tf_op jit(solution)/shard_map/reduce_scatter | solution.py:48
  1561.8 198.6 %all-gather.39.cloned.1.call-start = ((), (), s32[]{:S(2)}) async-start(), calls=%async_computation.25 | async-start | bytes 4456448 | tf_op jit(solution)/shard_map/all_gather | solution.py:12
  1643.7 202.5 %copy-start.3 = (f32[32,256]{1,0:T(8,128)S(1)}, f32[32,256]{1,0:T(8,128)}, u32[]{:S(2)}) copy-start(f32[32,256]{1,0:T(8,128)} %reduce-scatter.21.cloned.1.call-done) | copy-start | bytes 98308
  1684.6 161.5 %reduce-scatter.23.cloned.1.call-start = ((), (), s32[]{:S(2)}) async-start(), calls=%async_computation.15 | async-start | bytes 557056 | tf_op jit(solution)/shard_map/reduce_scatter | solution.py:48
Sparse Core Ops, SparseCore 0:
  54.2 74.4 all-gather.24
  131.3 103.0 all-gather.20
  237.1 102.8 all-gather.22
  347.7 81.5 reduce-scatter.8
  470.5 75.3 all-gather.26
  550.0 81.7 reduce-scatter.10
  673.0 75.1 all-gather.28
  752.3 81.8 reduce-scatter.12
  875.2 75.1 all-gather.30
  954.5 81.7 reduce-scatter.14
  1077.4 75.4 all-gather.32
  1157.0 81.7 reduce-scatter.16
  1280.0 75.0 all-gather.34
  1359.3 81.6 reduce-scatter.18
  1482.4 75.2 all-gather.36
  1561.9 81.7 reduce-scatter.20
  1684.7 75.5 all-gather.38
  1764.4 81.6 reduce-scatter.22
